TPU v7x, 256 devices: a whole 4x4x8 slice. The times are simulated.
256 devices in a mesh: crop: 2 (over y_hi), rows: 16 (over y_lo, x, core), hid: 8 (over z).
Axes of the slice: x: 4, y: 4 (y_hi: 2, y_lo: 2; y = y_hi * 2 + y_lo), z: 8, core: 2. Of those that a mesh axis runs over, the one named last changes fastest.
Arguments:
- tokens: bfloat16 [2, 32, 64, 4096], P('crop', 'rows', None, 'hid'), may hold values from -6 to 6
- cotangent: bfloat16 [2, 32, 64, 4096], P('crop', 'rows', None, 'hid'), may hold values from -6 to 6
- weight_in: bfloat16 [256, 64, 5, 256], P('rows', 'hid'), may hold values from -0.15625 to 0.15625
- weight_out: bfloat16 [256, 64, 5, 256], P('rows', 'hid'), may hold values from -0.078125 to 0.078125
- mix_kernel: float32 [9, 16384], P(None, 'hid'), may hold values from -4 to 4
- block_rows: int32 [64, 5], P('hid'), may hold values from 0 to 15, as said below
Outputs:
- grad_tokens: bfloat16 [2, 32, 64, 4096], P('crop', 'rows', None, 'hid')
- grad_w_in: float32 [256, 64, 5, 256], P(('crop', 'rows'), 'hid')
- grad_w_out: float32 [256, 64, 5, 256], P(('crop', 'rows'), 'hid')
- grad_kernel: float32 [9, 16384], P(None, 'hid')
Inputs may be any that keep to these rules, and one draw needn't show every extreme that they name: In each block column c, block_rows[c, 0] is a label L and block_rows[c, k] for k >= 1 is L with bit k - 1 flipped, so the 5 entries of a column differ; every value is the label of equally many block columns.
All inputs are finite; a program needn't handle non-finite values.
Results may differ from a plain program's by a relative error of at most 0.019.
Values may be sent and summed in bfloat16 or wider, within the bound.
No kernel may reach another device: no remote copies, remote signals or barrier semaphores. Data moves between devices by JAX's collectives and lax.ppermute only.
A program may use at most 128 MiB of HBM per device.

v0:
```python
import jax
import jax.numpy as jnp
from jax import lax
from jax.sharding import PartitionSpec as P

root_two_pi = 0.7978845608
cubic_coef = 0.044715
loss_scale = 0.03125


def padded(shard, sides, width):
    for axis, dim in sides:
        devices, length = (lax.axis_size(axis), shard.shape[dim])
        up = [(i, (i + 1) % devices) for i in range(devices - 1)]
        down = [(j, i) for i, j in up]
        last = lax.slice_in_dim(shard, length - width, length, axis=dim)
        initial = lax.slice_in_dim(shard, 0, width, axis=dim)
        before = lax.ppermute(last, axis, up)
        after = lax.ppermute(initial, axis, down)
        shard = jnp.concatenate([before, shard, after], axis=dim)
    return shard


def gelu_pair(preact):
    inner = root_two_pi * (preact + cubic_coef * preact * preact * preact)
    tanh_val = jnp.tanh(inner)
    gelu_out = 0.5 * preact * (1.0 + tanh_val)
    slopes = 0.5 * (1.0 + tanh_val) + 0.5 * preact * (1.0 - tanh_val * tanh_val) * root_two_pi * (
        1.0 + 3.0 * cubic_coef * preact * preact
    )
    return (gelu_out, slopes)


def on_device(tokens, cotangent, weight_in, weight_out, mix_kernel, block_rows):
    in_panel, out_panel = (
        lax.all_gather(weight_in, "rows", axis=0, tiled=True),
        lax.all_gather(weight_out, "rows", axis=0, tiled=True),
    )
    tok_full, cot_full = (
        lax.all_gather(tokens, "hid", axis=3, tiled=True),
        lax.all_gather(cotangent, "hid", axis=3, tiled=True),
    )
    crop_count, height, grid_width, depth_all = tok_full.shape
    tok_count = crop_count * height * grid_width
    block_size = in_panel.shape[0]
    col_count = in_panel.shape[1]
    nnz_count = in_panel.shape[2]
    block_count = depth_all // block_size
    hidden_local = col_count * block_size
    flat_rows = block_rows.reshape(-1)
    in_select = jnp.take(
        tok_full.reshape(tok_count, block_count, block_size), flat_rows, axis=1
    ).reshape(tok_count, col_count, nnz_count, block_size)
    grad_select = jnp.take(
        cot_full.reshape(tok_count, block_count, block_size), flat_rows, axis=1
    ).reshape(tok_count, col_count, nnz_count, block_size)
    pre_act = jnp.einsum("tckb,bcke->tce", in_select, in_panel, preferred_element_type=jnp.float32)
    gelu_out, slopes = gelu_pair(pre_act)
    active = gelu_out.astype(jnp.bfloat16).reshape(crop_count, height, grid_width, hidden_local)
    act_rim = padded(active, (("rows", 1),), 1)
    mix_grad = (
        jnp.einsum("tckd,fckd->tcf", grad_select, out_panel, preferred_element_type=jnp.float32)
        .astype(jnp.bfloat16)
        .reshape(crop_count, height, grid_width, hidden_local)
    )
    grad_rim = padded(mix_grad, (("rows", 1),), 1)
    act_pad = jnp.pad(act_rim.astype(jnp.float32), ((0, 0), (0, 0), (1, 1), (0, 0)))
    grad_pad = jnp.pad(grad_rim.astype(jnp.float32), ((0, 0), (0, 0), (1, 1), (0, 0)))
    grad_grid = mix_grad.astype(jnp.float32)
    mix_sum = jnp.zeros((crop_count, height, grid_width, hidden_local), jnp.float32)
    act_grad = jnp.zeros((crop_count, height, grid_width, hidden_local), jnp.float32)
    kern_terms = []
    for row_off in range(3):
        for col_off in range(3):
            tap = mix_kernel[3 * row_off + col_off]
            shifted = act_pad[:, row_off : row_off + height, col_off : col_off + grid_width]
            mix_sum = mix_sum + tap * shifted
            act_grad = (
                act_grad
                + tap
                * grad_pad[
                    :, 2 - row_off : 2 - row_off + height, 2 - col_off : 2 - col_off + grid_width
                ]
            )
            kern_terms.append(jnp.sum(shifted * grad_grid, axis=(0, 1, 2)))
    kern_local = jnp.stack(kern_terms, axis=0) * loss_scale
    mix_out = mix_sum.astype(jnp.bfloat16).reshape(tok_count, col_count, block_size)
    pre_grad = (act_grad.reshape(tok_count, col_count, block_size) * slopes).astype(jnp.bfloat16)
    kern_total = lax.psum(kern_local.astype(jnp.bfloat16), ("crop", "rows")).astype(jnp.float32)
    back_select = jnp.einsum(
        "tce,bcke->tckb", pre_grad, in_panel, preferred_element_type=jnp.float32
    )
    one_hot = (
        block_rows[:, :, None] == jnp.arange(block_count, dtype=jnp.int32)[None, None, :]
    ).astype(jnp.float32)
    token_terms = jnp.einsum(
        "tckb,ckr->trb", back_select, one_hot, precision=lax.Precision.HIGHEST
    ).reshape(crop_count, height, grid_width, depth_all)
    grad_tokens = lax.psum_scatter(
        token_terms.astype(jnp.bfloat16), "hid", scatter_dimension=3, tiled=True
    )
    first_term = jnp.einsum(
        "tckb,tce->bcke", in_select, pre_grad, preferred_element_type=jnp.float32
    )
    second_term = jnp.einsum(
        "tcf,tckd->fckd", mix_out, grad_select, preferred_element_type=jnp.float32
    )
    share_sums = lax.psum_scatter(
        (jnp.stack([first_term, second_term], axis=1) * loss_scale).astype(jnp.bfloat16),
        ("crop", "rows"),
        scatter_dimension=0,
        tiled=True,
    ).astype(jnp.float32)
    return (grad_tokens, share_sums[:, 0], share_sums[:, 1], kern_total)


def solution(mesh):
    placed = (
        P("crop", "rows", None, "hid"),
        P("crop", "rows", None, "hid"),
        P("rows", "hid", None, None),
        P("rows", "hid", None, None),
        P(None, "hid"),
        P("hid", None),
    )
    return jax.shard_map(
        on_device,
        mesh=mesh,
        in_specs=placed,
        out_specs=(
            P("crop", "rows", None, "hid"),
            P(("crop", "rows"), "hid", None, None),
            P(("crop", "rows"), "hid", None, None),
            P(None, "hid"),
        ),
        check_vma=False,
    )
```

profile of v0, /device:TPU:4, one launch (start us, length us, event | category | flops | bytes accessed | tf_op | source)
XLA Modules:
  0.0 380.4 jit_solution(11429003799002727429)
XLA Ops:
  7.2 0.7 all-gather.9.cloned.1.call-update
  7.9 0.7 all-gather.5.cloned.1.call-update
  8.7 1.8 copy.46
  10.5 1.8 copy.49
  12.4 0.8 reshape.183
  13.2 38.3 %all-gather.9.cloned.1.call-done = bf16[1,2,64,4096]{3,2,1,0:T(8,128)(2,1)} async-done(((bf16[1,2,64,512]{3,2,1,0:T(8,128)(2,1)}), bf16[1,2,64,4096]{3,2,1,0:T(8,128)(2,1)}) %all-gather.9.cloned.1.call-update) | async-done | bytes 1048592 | tf_op jit(solution)/shard_map/all_gather | solution.py:40
  51.5 1.5 copy.70
  53.0 0.3 copy.48
  53.3 37.1 %all-gather.5.cloned.1.call-done = bf16[1,2,64,4096]{3,2,1,0:T(8,128)(2,1)} async-done(((bf16[1,2,64,512]{3,2,1,0:T(8,128)(2,1)}), bf16[1,2,64,4096]{3,2,1,0:T(8,128)(2,1)}) %all-gather.5.cloned.1.call-update) | async-done | bytes 1048592 | tf_op jit(solution)/shard_map/all_gather | solution.py:41
  90.4 1.5 copy.68
  91.9 0.3 copy.45
  92.2 2.4 gather_fusion.1
  94.6 2.4 gather_fusion
  97.0 4.6 %broadcast_select_fusion.1 = (bf16[40,128,256]{2,1,0:T(8,128)(2,1)S(1)}, bf16[40,128,256]{2,1,0:T(8,128)(2,1)}) fusion(bf16[40,128,256]{2,1,0:T(8,128)(2,1)} %gather_fusion, pred[40]{0:T(512)(128)(4,1)S(1)} %compare_and_fusion, bf16[40,128,256]{2,1,0:T(8,128)(2,1)} %gather_fusion.1), kind=kLoop, calls=%fused_computation.18 | loop fusion | flops 2621440 | bytes 10485800 | tf_op jit(solution)/shard_map/jit(_take)/select_n | solution.py:54
  101.6 30.2 %all-gather.7.cloned.1.call-done = bf16[256,8,5,256]{3,0,2,1:T(8,128)(2,1)} async-done(((bf16[16,8,5,256]{3,0,2,1:T(8,128)(2,1)}), bf16[256,8,5,256]{3,0,2,1:T(8,128)(2,1)}) %all-gather.7.cloned.1.call-update) | async-done | bytes 5242896 | tf_op jit(solution)/shard_map/all_gather | solution.py:37
  131.8 4.3 %fusion.9 = bf16[128,8,256]{2,0,1:T(8,128)(2,1)S(1)} fusion(bf16[128,8,5,256]{3,0,2,1:T(8,128)(2,1)S(1)} %bitcast.97, bf16[256,8,5,256]{3,0,2,1:T(8,128)(2,1)} %all-gather.7.cloned.1.call-done), kind=kOutput, calls=%fused_computation.39 | convolution fusion | flops 671350784 | bytes 8388608 | tf_op jit(solution)/shard_map/tckd,fckd->tcf/dot_general | solution.py:62
  136.2 1.1 copy.47
  137.2 1.3 reshape.185
  138.6 2.1 collective-permute-start
  140.7 3.4 collective-permute-start.1
  144.2 2.0 collective-permute-done
  146.3 3.6 collective-permute-done.1
  150.0 0.9 fusion.25
  150.9 1.3 copy.69
  152.2 25.9 %all-gather.11.cloned.1.call-done = bf16[256,8,5,256]{3,0,2,1:T(8,128)(2,1)} async-done(((bf16[16,8,5,256]{3,0,2,1:T(8,128)(2,1)}), bf16[256,8,5,256]{3,0,2,1:T(8,128)(2,1)}) %all-gather.11.cloned.1.call-update) | async-done | bytes 5242896 | tf_op jit(solution)/shard_map/all_gather | solution.py:36
  178.1 5.1 %multiply_convert_fusion = (bf16[128,8,256]{2,0,1:T(8,128)(2,1)S(1)}, bf16[128,8,256]{2,0,1:T(8,128)(2,1)}) fusion(f32[128,8,256]{2,1,0:T(8,128)} %bitcast.108, bf16[128,8,5,256]{3,0,2,1:T(8,128)(2,1)S(1)} %bitcast.99, bf16[256,8,5,256]{3,0,2,1:T(8,128)(2,1)} %all-gather.11.cloned.1.call-done), kind=kOutput, calls=%fused_computation.76 | convolution fusion | flops 676593664 | bytes 9961472 | tf_op jit(solution)/shard_map/tckb,bcke->tce/dot_general | solution.py:57
  183.3 1.1 copy.53
  184.4 2.1 reshape.189
  186.5 1.1 fusion.46
  187.5 2.1 collective-permute-start.2
  189.7 3.6 collective-permute-start.3
  193.3 2.7 convolution_bitcast_fusion.1
  196.0 1.0 collective-permute-done.3
  197.2 0.9 add_convert_fusion
  198.2 0.7 copy-done.1
  198.9 1.6 convolution_bitcast_fusion
  200.5 5.7 %fusion = bf16[256,2,8,5,256]{0,4,3,2,1:T(8,128)(2,1)} fusion(f32[256,1,8,5,256]{0,4,3,2,1:T(8,128)S(1)} %convolution_bitcast_fusion, f32[256,1,8,5,256]{0,4,3,2,1:T(8,128)S(1)} %convolution_bitcast_fusion.1), kind=kLoop, calls=%fused_computation.3 | loop fusion | flops 15728640 | bytes 31457280 | tf_op jit(solution)/shard_map/convert_element_type | solution.py:109
  206.2 15.4 %copy.56 = bf16[256,2,8,5,256]{4,2,3,1,0:T(8,128)(2,1)} copy(bf16[256,2,8,5,256]{0,4,3,2,1:T(8,128)(2,1)} %fusion) | data formatting | bytes 20971520 | tf_op jit(solution)/shard_map/convert_element_type | solution.py:109
  221.9 0.4 copy-done.6
  222.6 4.3 %convolution_bitcast_fusion.2 = f32[128,8,5,256]{3,0,2,1:T(8,128)S(1)} fusion(bf16[256,8,5,256]{3,0,2,1:T(8,128)(2,1)} %all-gather.11.cloned.1.call-done, bf16[128,8,256]{2,0,1:T(8,128)(2,1)S(1)} %copy-done.4), kind=kOutput, calls=%fused_computation.19 | convolution fusion | flops 671088640 | bytes 11010048 | tf_op jit(solution)/shard_map/tce,bcke->tckb/dot_general | solution.py:90
  227.0 5.9 %fusion.5 = bf16[128,16,256]{2,1,0:T(8,128)(2,1)} fusion(f32[128,8,5,256]{3,0,2,1:T(8,128)S(1)} %convolution_bitcast_fusion.2, s32[8,5]{0,1:T(8,128)S(1)} %copy.44), kind=kOutput, calls=%fused_computation.35 | convolution fusion | flops 252183168 | bytes 6291616 | tf_op jit(solution)/shard_map/tckb,ckr->trb/dot_general | solution.py:96
  232.8 2.3 convert_element_type.87
  235.2 1.0 fusion.39
  236.4 117.1 %psum.7 = bf16[9,2048]{1,0:T(8,128)(2,1)S(1)} all-reduce(bf16[9,2048]{1,0:T(8,128)(2,1)S(1)} %multiply_convert_fusion.1), channel_id=1, replica_groups=mesh['crop'=2,'rows'=16,'hid'=8] {'crop','rows'}, use_global_device_ids=true, to_apply=%region_11.13 | all-reduce | flops 18432 | bytes 73728 | tf_op jit(solution)/shard_map/psum | solution.py:89
  353.5 0.7 convert_element_type.95
  354.2 1.0 convert_element_type.92
  355.2 0.9 slice_bitcast_fusion
  356.1 17.5 %reduce-scatter.3.cloned.1.call-done = bf16[1,2,64,512]{3,2,1,0:T(8,128)(2,1)} async-done(((bf16[1,2,64,4096]{3,2,1,0:T(8,128)(2,1)}), bf16[1,2,64,512]{3,2,1,0:T(8,128)(2,1)}) %reduce-scatter.3.cloned.1.call-update) | async-done | bytes 131088 | tf_op jit(solution)/shard_map/reduce_scatter | solution.py:99
  (35 shorter events, 1.6 us)
Async XLA Ops:
  7.2 44.3 %all-gather.9.cloned.1.call-start = ((), (), s32[]{:S(2)}) async-start(), calls=%async_computation.4 | async-start | bytes 1179648 | tf_op jit(solution)/shard_map/all_gather | solution.py:40
  7.9 82.5 %all-gather.5.cloned.1.call-start = ((), (), s32[]{:S(2)}) async-start(), calls=%async_computation.2 | async-start | bytes 1179648 | tf_op jit(solution)/shard_map/all_gather | solution.py:41
  8.6 123.2 %all-gather.7.cloned.1.call-start = ((), (), s32[]{:S(2)}) async-start(), calls=%async_computation.3 | async-start | bytes 5570560 | tf_op jit(solution)/shard_map/all_gather | solution.py:37
  10.5 167.7 %all-gather.11.cloned.1.call-start = ((), (), s32[]{:S(2)}) async-start(), calls=%async_computation.5 | async-start | bytes 5570560 | tf_op jit(solution)/shard_map/all_gather | solution.py:36
  12.3 341.8 %reduce-scatter.5.cloned.1.call-start = ((), (), s32[]{:S(2)}) async-start(), calls=%async_computation.7 | async-start | bytes 10813440 | tf_op jit(solution)/shard_map/reduce_scatter | solution.py:108
  101.6 34.5 %copy-start = (bf16[40,128,256]{2,1,0:T(8,128)(2,1)}, bf16[40,128,256]{2,1,0:T(8,128)(2,1)S(1)}, u32[]{:S(2)}) copy-start(bf16[40,128,256]{2,1,0:T(8,128)(2,1)S(1)} %get-tuple-element.43) | copy-start | bytes 7864324
  136.1 8.0 %copy-start.5 = (f32[9,2048]{1,0:T(8,128)S(1)}, f32[9,2048]{1,0:T(8,128)}, u32[]{:S(2)}) copy-start(f32[9,2048]{1,0:T(8,128)} %param.12) | copy-start | bytes 221188
  138.6 7.7 %collective-permute-start = (bf16[1,1,64,2048]{3,2,1,0:T(8,128)(2,1)S(1)}, bf16[1,1,64,2048]{3,2,1,0:T(8,128)(2,1)S(1)}, u32[]{:S(2)}, u32[]{:S(2)}) collective-permute-start(bf16[1,1,64,2048]{3,2,1,0:T(8,128)(2,1)S(1)} %get-tuple-element.32), channel_id=1, source_target_pairs={{0,8},{8,16},{16,24},{24,32},{32,40},{40,48},{48,56},{56,64},{64,7... | collective-permute-start | bytes 786440 | tf_op jit(solution)/shard_map/ppermute | solution.py:18
  140.7 9.2 %collective-permute-start.1 = (bf16[1,1,64,2048]{3,2,1,0:T(8,128)(2,1)S(1)}, bf16[1,1,64,2048]{3,2,1,0:T(8,128)(2,1)S(1)}, u32[]{:S(2)}, u32[]{:S(2)}) collective-permute-start(bf16[1,1,64,2048]{3,2,1,0:T(8,128)(2,1)S(1)} %get-tuple-element.33), channel_id=1, source_target_pairs={{8,0},{16,8},{24,16},{32,24},{40,32},{48,40},{56,48},{64,56},{72,6... | collective-permute-start | bytes 786440 | tf_op jit(solution)/shard_map/ppermute | solution.py:19
  150.0 28.1 %copy-start.2 = (bf16[40,128,256]{2,1,0:T(8,128)(2,1)S(1)}, bf16[40,128,256]{2,1,0:T(8,128)(2,1)}, u32[]{:S(2)}) copy-start(bf16[40,128,256]{2,1,0:T(8,128)(2,1)} %get-tuple-element.44) | copy-start | bytes 7864324
  187.5 8.4 %collective-permute-start.2 = (bf16[1,1,64,2048]{3,2,1,0:T(8,128)(2,1)S(1)}, bf16[1,1,64,2048]{3,2,1,0:T(8,128)(2,1)S(1)}, u32[]{:S(2)}, u32[]{:S(2)}) collective-permute-start(bf16[1,1,64,2048]{3,2,1,0:T(8,128)(2,1)S(1)} %get-tuple-element.30), channel_id=1, source_target_pairs={{0,8},{8,16},{16,24},{24,32},{32,40},{40,48},{48,56},{56,64},{64,7... | collective-permute-start | bytes 786440 | tf_op jit(solution)/shard_map/ppermute | solution.py:18
  189.7 7.3 %collective-permute-start.3 = (bf16[1,1,64,2048]{3,2,1,0:T(8,128)(2,1)S(1)}, bf16[1,1,64,2048]{3,2,1,0:T(8,128)(2,1)S(1)}, u32[]{:S(2)}, u32[]{:S(2)}) collective-permute-start(bf16[1,1,64,2048]{3,2,1,0:T(8,128)(2,1)S(1)} %get-tuple-element.31), channel_id=1, source_target_pairs={{8,0},{16,8},{24,16},{32,24},{40,32},{48,40},{56,48},{64,56},{72,6... | collective-permute-start | bytes 786440 | tf_op jit(solution)/shard_map/ppermute | solution.py:19
  193.3 3.7 copy-start.3
  197.2 1.7 copy-start.1
  221.6 0.7 copy-start.6
  221.6 1.1 copy-start.4
  221.6 152.0 %reduce-scatter.3.cloned.1.call-start = ((), (), s32[]{:S(2)}) async-start(), calls=%async_computation.6 | async-start | bytes 1179648 | tf_op jit(solution)/shard_map/reduce_scatter | solution.py:99
Sparse Core Ops, SparseCore 0:
  9.8 41.6 all-gather.8
  53.3 37.0 all-gather.4
  92.8 39.0 all-gather.6
  134.0 44.0 all-gather.10
  221.7 110.2 reduce-scatter.4
  335.1 38.3 reduce-scatter.2
where the time goes:
time: 381 us; the launch traced here: 380 us
  waiting for transfers between devices  157 us (41%)
  blocking collectives  117 us (31%)
  local copies, waits for them, and re-layouts  41.1 us (11%)
  matrix products  23.8 us (6%)
  other arithmetic  15.2 us (4%)
  between operations  14.3 us (4%)
  starting transfers between devices  11.8 us (3%)
    psum x1, blocking collectives, on_device(): lax.psum(kern_local.astype(jnp.bfloat16), ('crop', 'rows'))  117 us
    all_gather x1, waiting for transfers between devices, on_device(): lax.all_gather(tokens, 'hid', axis=3, tiled=True)  38.3 us
    all_gather x1, waiting for transfers between devices, on_device(): lax.all_gather(cotangent, 'hid', axis=3, tiled=True)  37.1 us
    all_gather x1, waiting for transfers between devices, on_device(): lax.all_gather(weight_out, 'rows', axis=0, tiled=True)  30.2 us
    all_gather x1, waiting for transfers between devices, on_device(): lax.all_gather(weight_in, 'rows', axis=0, tiled=True)  25.9 us
    reduce_scatter x1, waiting for transfers between devices, on_device(): lax.psum_scatter(token_terms.astype(jnp.bfloat16), 'hid', scatter_dimensi...  17.5 us
    convert_element_type x1, local copies, waits for them, and re-layouts, on_device(): (jnp.stack([first_term, second_term], axis=1) * loss_scale).astype(jnp.bf...  15.4 us
    unnamed x21, local copies, waits for them, and re-layouts  9.42 us
  transfers between devices with their start and end apart: 10, of which 8 were waited for; matrix products, arithmetic and copies ran while one was open for 12% of the time, Pallas kernels for 0%

commit v1 on v0

--- a/solution.py
+++ b/solution.py
@@ -36,10 +36,30 @@
         lax.all_gather(weight_in, "rows", axis=0, tiled=True),
         lax.all_gather(weight_out, "rows", axis=0, tiled=True),
     )
-    tok_full, cot_full = (
-        lax.all_gather(tokens, "hid", axis=3, tiled=True),
-        lax.all_gather(cotangent, "hid", axis=3, tiled=True),
-    )
+
+    def _carry_desk(chunk):
+        peer_axis = "hid"
+        left_arr = lax.axis_size(peer_axis)
+        high, outer, f_now = (left_arr, lax.axis_index(peer_axis), chunk.shape[3])
+        panels = [(w, (w + 1) % high) for w in range(high)]
+        samples = [(w, (w - 1) % high) for w in range(high)]
+        top = jnp.zeros((*chunk.shape[:3], high * f_now, *chunk.shape[4:]), chunk.dtype)
+        upper = g_now = chunk
+        h_now = high // 2
+        h = 1
+        top = lax.dynamic_update_slice_in_dim(top, chunk, outer * f_now, axis=3)
+        while h < h_now + 1:
+            upper = lax.ppermute(upper, axis_name=peer_axis, perm=panels)
+            top = lax.dynamic_update_slice_in_dim(top, upper, (outer - h) % high * f_now, axis=3)
+            if h < high - h_now:
+                g_now = lax.ppermute(g_now, peer_axis, samples)
+                top = lax.dynamic_update_slice_in_dim(
+                    top, g_now, (outer + h) % high * f_now, axis=3
+                )
+            h += 1
+        return top
+
+    tok_full, cot_full = (_carry_desk(tokens), lax.all_gather(cotangent, "hid", axis=3, tiled=True))
     crop_count, height, grid_width, depth_all = tok_full.shape
     tok_count = crop_count * height * grid_width
     block_size = in_panel.shape[0]

time: 381 us -> 343 us (0.900)
  waiting for transfers between devices: 157 us -> 107 us
  starting transfers between devices: 11.8 us -> 24.9 us
    all_gather x1 -> x0, waiting for transfers between devices: 38.3 us -> none  [on_device(): lax.all_gather(tokens, 'hid', axis=3, tiled=True)]
    all_gather x1, waiting for transfers between devices: 37.1 us -> 3.63 us  [on_device(): lax.all_gather(cotangent, 'hid', axis=3, tiled=True)]
    ppermute x0 -> x7, waiting for transfers between devices: none -> 19.7 us  [the longest x4 14.4 us: _carry_desk(): upper = lax.ppermute(upper, axis_name=peer_axis, perm=panels)]
    ppermute x0 -> x7, starting transfers between devices: none -> 13.2 us  [the longest x3 13.2 us: _carry_desk(): g_now = lax.ppermute(g_now, peer_axis, samples)]
    unnamed x21 -> x23, local copies, waits for them, and re-layouts: 9.42 us -> 8.19 us
  transfers between devices with their start and end apart: 10 -> 16, of which waited for: 8 -> 11; matrix products, arithmetic and copies ran while one was open for 12% -> 13% of each run, Pallas kernels for 0% -> 0%
where the time goes in v1:
time: 343 us; the launch traced here: 342 us
  blocking collectives  117 us (34%)
  waiting for transfers between devices  107 us (31%)
  local copies, waits for them, and re-layouts  40 us (12%)
  starting transfers between devices  24.9 us (7%)
  matrix products  23.8 us (7%)
  other arithmetic  15.1 us (4%)
  between operations  14.2 us (4%)
    psum x1, blocking collectives, on_device(): lax.psum(kern_local.astype(jnp.bfloat16), ('crop', 'rows'))  117 us
    all_gather x1, waiting for transfers between devices, on_device(): lax.all_gather(weight_out, 'rows', axis=0, tiled=True)  32.3 us
    all_gather x1, waiting for transfers between devices, on_device(): lax.all_gather(weight_in, 'rows', axis=0, tiled=True)  26.4 us
    reduce_scatter x1, waiting for transfers between devices, on_device(): lax.psum_scatter(token_terms.astype(jnp.bfloat16), 'hid', scatter_dimensi...  17.4 us
    convert_element_type x1, local copies, waits for them, and re-layouts, on_device(): (jnp.stack([first_term, second_term], axis=1) * loss_scale).astype(jnp.bf...  15.4 us
    ppermute x4, waiting for transfers between devices, _carry_desk(): upper = lax.ppermute(upper, axis_name=peer_axis, perm=panels)  14.4 us
    ppermute x3, starting transfers between devices, _carry_desk(): g_now = lax.ppermute(g_now, peer_axis, samples)  13.2 us
    unnamed x23, local copies, waits for them, and re-layouts  8.19 us
  transfers between devices with their start and end apart: 16, of which 11 were waited for; matrix products, arithmetic and copies ran while one was open for 13% of the time, Pallas kernels for 0%

profile of v1, /device:TPU:4, one launch (start us, length us, event | category | flops | bytes accessed | tf_op | source)
XLA Modules:
  0.0 341.8 jit_solution(3259652234687622958)
XLA Ops:
  7.2 0.7 all-gather.4.cloned.1.call-update
  8.0 1.8 copy.45
  9.8 1.8 copy.48
  11.6 5.9 %collective-permute-start.3 = (bf16[1,2,64,512]{3,2,1,0:T(8,128)(2,1)}, bf16[1,2,64,512]{3,2,1,0:T(8,128)(2,1)S(1)}, u32[]{:S(2)}, u32[]{:S(2)}) collective-permute-start(bf16[1,2,64,512]{3,2,1,0:T(8,128)(2,1)} %param.8), channel_id=1, source_target_pairs={{0,7},{1,0},{2,1},{3,2},{4,3},{5,4},{6,5},{7,6},{8,15},{9,8},{10,9... | collective-permute-start | bytes 393224 | tf_op jit(solution)/shard_map/ppermute | solution.py:55
  17.6 0.8 reshape.183
  18.6 2.0 collective-permute-done.3
  20.6 3.6 %collective-permute-start.5 = (bf16[1,2,64,512]{3,2,1,0:T(8,128)(2,1)S(1)}, bf16[1,2,64,512]{3,2,1,0:T(8,128)(2,1)S(1)}, u32[]{:S(2)}, u32[]{:S(2)}) collective-permute-start(bf16[1,2,64,512]{3,2,1,0:T(8,128)(2,1)S(1)} %collective-permute-done.3), channel_id=1, source_target_pairs={{0,7},{1,0},{2,1},{3,2},{4,3},{5,4},{6,5},{7,6},{8,15},{9,8},{10,9... | collective-permute-start | bytes 393224 | tf_op jit(solution)/shard_map/ppermute | solution.py:55
  24.3 3.2 collective-permute-done.5
  27.5 3.7 %collective-permute-start.7 = (bf16[1,2,64,512]{3,2,1,0:T(8,128)(2,1)S(1)}, bf16[1,2,64,512]{3,2,1,0:T(8,128)(2,1)S(1)}, u32[]{:S(2)}, u32[]{:S(2)}) collective-permute-start(bf16[1,2,64,512]{3,2,1,0:T(8,128)(2,1)S(1)} %collective-permute-done.5), channel_id=1, source_target_pairs={{0,7},{1,0},{2,1},{3,2},{4,3},{5,4},{6,5},{7,6},{8,15},{9,8},{10,9... | collective-permute-start | bytes 393224 | tf_op jit(solution)/shard_map/ppermute | solution.py:55
  31.2 7.2 %collective-permute-done.6 = bf16[1,2,64,512]{3,2,1,0:T(8,128)(2,1)S(1)} collective-permute-done((bf16[1,2,64,512]{3,2,1,0:T(8,128)(2,1)S(1)}, bf16[1,2,64,512]{3,2,1,0:T(8,128)(2,1)S(1)}, u32[]{:S(2)}, u32[]{:S(2)}) %collective-permute-start.6) | collective-permute-done | bytes 131104 | tf_op jit(solution)/shard_map/ppermute | solution.py:52
  38.5 7.2 %collective-permute-done.8 = bf16[1,2,64,512]{3,2,1,0:T(8,128)(2,1)S(1)} collective-permute-done((bf16[1,2,64,512]{3,2,1,0:T(8,128)(2,1)S(1)}, bf16[1,2,64,512]{3,2,1,0:T(8,128)(2,1)S(1)}, u32[]{:S(2)}, u32[]{:S(2)}) %collective-permute-start.8) | collective-permute-done | bytes 131104 | tf_op jit(solution)/shard_map/ppermute | solution.py:52
  46.3 2.4 gather_fusion.1
  48.7 3.6 %all-gather.4.cloned.1.call-done = bf16[1,2,64,4096]{3,2,1,0:T(8,128)(2,1)} async-done(((bf16[1,2,64,512]{3,2,1,0:T(8,128)(2,1)}), bf16[1,2,64,4096]{3,2,1,0:T(8,128)(2,1)}) %all-gather.4.cloned.1.call-update) | async-done | bytes 1048592 | tf_op jit(solution)/shard_map/all_gather | solution.py:62
  52.3 1.5 copy.67
  54.1 2.4 gather_fusion
  56.6 4.6 %broadcast_select_fusion.1 = (bf16[40,128,256]{2,1,0:T(8,128)(2,1)S(1)}, bf16[40,128,256]{2,1,0:T(8,128)(2,1)}) fusion(bf16[40,128,256]{2,1,0:T(8,128)(2,1)} %gather_fusion, pred[40]{0:T(512)(128)(4,1)S(1)} %compare_and_fusion, bf16[40,128,256]{2,1,0:T(8,128)(2,1)} %gather_fusion.1), kind=kLoop, calls=%fused_computation.18 | loop fusion | flops 2621440 | bytes 10485800 | tf_op jit(solution)/shard_map/jit(_take)/select_n | solution.py:74
  61.2 32.3 %all-gather.6.cloned.1.call-done = bf16[256,8,5,256]{3,0,2,1:T(8,128)(2,1)} async-done(((bf16[16,8,5,256]{3,0,2,1:T(8,128)(2,1)}), bf16[256,8,5,256]{3,0,2,1:T(8,128)(2,1)}) %all-gather.6.cloned.1.call-update) | async-done | bytes 5242896 | tf_op jit(solution)/shard_map/all_gather | solution.py:37
  93.5 4.3 %fusion.9 = bf16[128,8,256]{2,0,1:T(8,128)(2,1)S(1)} fusion(bf16[128,8,5,256]{3,0,2,1:T(8,128)(2,1)S(1)} %bitcast.97, bf16[256,8,5,256]{3,0,2,1:T(8,128)(2,1)} %all-gather.6.cloned.1.call-done), kind=kOutput, calls=%fused_computation.39 | convolution fusion | flops 671350784 | bytes 8388608 | tf_op jit(solution)/shard_map/tckd,fckd->tcf/dot_general | solution.py:82
  97.8 1.1 copy.46
  98.9 1.3 reshape.185
  100.3 2.1 collective-permute-start
  102.4 3.6 %collective-permute-start.1 = (bf16[1,1,64,2048]{3,2,1,0:T(8,128)(2,1)S(1)}, bf16[1,1,64,2048]{3,2,1,0:T(8,128)(2,1)S(1)}, u32[]{:S(2)}, u32[]{:S(2)}) collective-permute-start(bf16[1,1,64,2048]{3,2,1,0:T(8,128)(2,1)S(1)} %get-tuple-element.33), channel_id=1, source_target_pairs={{8,0},{16,8},{24,16},{32,24},{40,32},{48,40},{56,48},{64,56},{72,6... | collective-permute-start | bytes 786440 | tf_op jit(solution)/shard_map/ppermute | solution.py:19
  106.1 1.9 collective-permute-done
  107.9 3.3 collective-permute-done.1
  111.4 0.9 fusion.25
  112.3 1.3 copy.68
  113.6 26.4 %all-gather.8.cloned.1.call-done = bf16[256,8,5,256]{3,0,2,1:T(8,128)(2,1)} async-done(((bf16[16,8,5,256]{3,0,2,1:T(8,128)(2,1)}), bf16[256,8,5,256]{3,0,2,1:T(8,128)(2,1)}) %all-gather.8.cloned.1.call-update) | async-done | bytes 5242896 | tf_op jit(solution)/shard_map/all_gather | solution.py:36
  140.0 5.1 %multiply_convert_fusion = (bf16[128,8,256]{2,0,1:T(8,128)(2,1)S(1)}, bf16[128,8,256]{2,0,1:T(8,128)(2,1)}) fusion(f32[128,8,256]{2,1,0:T(8,128)} %bitcast.108, bf16[128,8,5,256]{3,0,2,1:T(8,128)(2,1)S(1)} %bitcast.99, bf16[256,8,5,256]{3,0,2,1:T(8,128)(2,1)} %all-gather.8.cloned.1.call-done), kind=kOutput, calls=%fused_computation.76 | convolution fusion | flops 676593664 | bytes 9961472 | tf_op jit(solution)/shard_map/tckb,bcke->tce/dot_general | solution.py:77
  145.1 1.1 copy.52
  146.2 2.1 reshape.189
  148.3 1.1 fusion.46
  149.3 2.1 collective-permute-start.9
  151.5 3.4 %collective-permute-start.10 = (bf16[1,1,64,2048]{3,2,1,0:T(8,128)(2,1)S(1)}, bf16[1,1,64,2048]{3,2,1,0:T(8,128)(2,1)S(1)}, u32[]{:S(2)}, u32[]{:S(2)}) collective-permute-start(bf16[1,1,64,2048]{3,2,1,0:T(8,128)(2,1)S(1)} %get-tuple-element.31), channel_id=1, source_target_pairs={{8,0},{16,8},{24,16},{32,24},{40,32},{48,40},{56,48},{64,56},{72,6... | collective-permute-start | bytes 786440 | tf_op jit(solution)/shard_map/ppermute | solution.py:19
  154.9 2.7 convolution_bitcast_fusion.1
  157.6 1.2 collective-permute-done.10
  159.0 0.9 add_convert_fusion
  160.0 0.7 copy-done.1
  160.7 1.6 convolution_bitcast_fusion
  162.3 5.7 %fusion = bf16[256,2,8,5,256]{0,4,3,2,1:T(8,128)(2,1)} fusion(f32[256,1,8,5,256]{0,4,3,2,1:T(8,128)S(1)} %convolution_bitcast_fusion, f32[256,1,8,5,256]{0,4,3,2,1:T(8,128)S(1)} %convolution_bitcast_fusion.1), kind=kLoop, calls=%fused_computation.3 | loop fusion | flops 15728640 | bytes 31457280 | tf_op jit(solution)/shard_map/convert_element_type | solution.py:129
  167.9 15.4 %copy.55 = bf16[256,2,8,5,256]{4,2,3,1,0:T(8,128)(2,1)} copy(bf16[256,2,8,5,256]{0,4,3,2,1:T(8,128)(2,1)} %fusion) | data formatting | bytes 20971520 | tf_op jit(solution)/shard_map/convert_element_type | solution.py:129
  184.4 4.3 %convolution_bitcast_fusion.2 = f32[128,8,5,256]{3,0,2,1:T(8,128)S(1)} fusion(bf16[256,8,5,256]{3,0,2,1:T(8,128)(2,1)} %all-gather.8.cloned.1.call-done, bf16[128,8,256]{2,0,1:T(8,128)(2,1)S(1)} %copy-done.4), kind=kOutput, calls=%fused_computation.19 | convolution fusion | flops 671088640 | bytes 11010048 | tf_op jit(solution)/shard_map/tce,bcke->tckb/dot_general | solution.py:110
  188.7 5.9 %fusion.5 = bf16[128,16,256]{2,1,0:T(8,128)(2,1)} fusion(f32[128,8,5,256]{3,0,2,1:T(8,128)S(1)} %convolution_bitcast_fusion.2, s32[8,5]{0,1:T(8,128)S(1)} %copy.43), kind=kOutput, calls=%fused_computation.35 | convolution fusion | flops 252183168 | bytes 6291616 | tf_op jit(solution)/shard_map/tckb,ckr->trb/dot_general | solution.py:116
  194.5 2.3 convert_element_type.87
  196.9 1.0 fusion.39
  198.1 117.1 %psum.7 = bf16[9,2048]{1,0:T(8,128)(2,1)S(1)} all-reduce(bf16[9,2048]{1,0:T(8,128)(2,1)S(1)} %multiply_convert_fusion.1), channel_id=1, replica_groups=mesh['crop'=2,'rows'=16,'hid'=8] {'crop','rows'}, use_global_device_ids=true, to_apply=%region_11.13 | all-reduce | flops 18432 | bytes 73728 | tf_op jit(solution)/shard_map/psum | solution.py:109
  315.9 1.0 convert_element_type.92
  316.9 0.9 slice_bitcast_fusion
  317.8 17.4 %reduce-scatter.3.cloned.1.call-done = bf16[1,2,64,512]{3,2,1,0:T(8,128)(2,1)} async-done(((bf16[1,2,64,4096]{3,2,1,0:T(8,128)(2,1)}), bf16[1,2,64,512]{3,2,1,0:T(8,128)(2,1)}) %reduce-scatter.3.cloned.1.call-update) | async-done | bytes 131088 | tf_op jit(solution)/shard_map/reduce_scatter | solution.py:119
  (57 shorter events, 3.8 us)
Async XLA Ops:
  7.2 11.4 %copy-start.5 = (bf16[1,2,64,512]{3,2,1,0:T(8,128)(2,1)S(1)}, bf16[1,2,64,512]{3,2,1,0:T(8,128)(2,1)}, u32[]{:S(2)}) copy-start(bf16[1,2,64,512]{3,2,1,0:T(8,128)(2,1)} %param.8) | copy-start | bytes 393220
  7.2 45.1 %all-gather.4.cloned.1.call-start = ((), (), s32[]{:S(2)}) async-start(), calls=%async_computation.2 | async-start | bytes 1179648 | tf_op jit(solution)/shard_map/all_gather | solution.py:62
  7.9 85.6 %all-gather.6.cloned.1.call-start = ((), (), s32[]{:S(2)}) async-start(), calls=%async_computation.3 | async-start | bytes 5570560 | tf_op jit(solution)/shard_map/all_gather | solution.py:37
  9.7 130.2 %all-gather.8.cloned.1.call-start = ((), (), s32[]{:S(2)}) async-start(), calls=%async_computation.4 | async-start | bytes 5570560 | tf_op jit(solution)/shard_map/all_gather | solution.py:36
  11.6 304.3 %reduce-scatter.5.cloned.1.call-start = ((), (), s32[]{:S(2)}) async-start(), calls=%async_computation.6 | async-start | bytes 10813440 | tf_op jit(solution)/shard_map/reduce_scatter | solution.py:128
  11.6 9.0 %collective-permute-start.3 = (bf16[1,2,64,512]{3,2,1,0:T(8,128)(2,1)}, bf16[1,2,64,512]{3,2,1,0:T(8,128)(2,1)S(1)}, u32[]{:S(2)}, u32[]{:S(2)}) collective-permute-start(bf16[1,2,64,512]{3,2,1,0:T(8,128)(2,1)} %param.8), channel_id=1, source_target_pairs={{0,7},{1,0},{2,1},{3,2},{4,3},{5,4},{6,5},{7,6},{8,15},{9,8},{10,9... | collective-permute-start | bytes 393224 | tf_op jit(solution)/shard_map/ppermute | solution.py:55
  17.6 6.7 %collective-permute-start.2 = (bf16[1,2,64,512]{3,2,1,0:T(8,128)(2,1)}, bf16[1,2,64,512]{3,2,1,0:T(8,128)(2,1)S(1)}, u32[]{:S(2)}, u32[]{:S(2)}) collective-permute-start(bf16[1,2,64,512]{3,2,1,0:T(8,128)(2,1)} %param.8), channel_id=1, source_target_pairs={{0,1},{1,2},{2,3},{3,4},{4,5},{5,6},{6,7},{7,0},{8,9},{9,10},{10,1... | collective-permute-start | bytes 393224 | tf_op jit(solution)/shard_map/ppermute | solution.py:52
  20.6 6.9 %collective-permute-start.5 = (bf16[1,2,64,512]{3,2,1,0:T(8,128)(2,1)S(1)}, bf16[1,2,64,512]{3,2,1,0:T(8,128)(2,1)S(1)}, u32[]{:S(2)}, u32[]{:S(2)}) collective-permute-start(bf16[1,2,64,512]{3,2,1,0:T(8,128)(2,1)S(1)} %collective-permute-done.3), channel_id=1, source_target_pairs={{0,7},{1,0},{2,1},{3,2},{4,3},{5,4},{6,5},{7,6},{8,15},{9,8},{10,9... | collective-permute-start | bytes 393224 | tf_op jit(solution)/shard_map/ppermute | solution.py:55
  24.2 7.0 %collective-permute-start.4 = (bf16[1,2,64,512]{3,2,1,0:T(8,128)(2,1)S(1)}, bf16[1,2,64,512]{3,2,1,0:T(8,128)(2,1)S(1)}, u32[]{:S(2)}, u32[]{:S(2)}) collective-permute-start(bf16[1,2,64,512]{3,2,1,0:T(8,128)(2,1)S(1)} %collective-permute-done.2), channel_id=1, source_target_pairs={{0,1},{1,2},{2,3},{3,4},{4,5},{5,6},{6,7},{7,0},{8,9},{9,10},{10,1... | collective-permute-start | bytes 393224 | tf_op jit(solution)/shard_map/ppermute | solution.py:52
  27.5 11.0 %collective-permute-start.7 = (bf16[1,2,64,512]{3,2,1,0:T(8,128)(2,1)S(1)}, bf16[1,2,64,512]{3,2,1,0:T(8,128)(2,1)S(1)}, u32[]{:S(2)}, u32[]{:S(2)}) collective-permute-start(bf16[1,2,64,512]{3,2,1,0:T(8,128)(2,1)S(1)} %collective-permute-done.5), channel_id=1, source_target_pairs={{0,7},{1,0},{2,1},{3,2},{4,3},{5,4},{6,5},{7,6},{8,15},{9,8},{10,9... | collective-permute-start | bytes 393224 | tf_op jit(solution)/shard_map/ppermute | solution.py:55
  31.2 7.3 %collective-permute-start.6 = (bf16[1,2,64,512]{3,2,1,0:T(8,128)(2,1)S(1)}, bf16[1,2,64,512]{3,2,1,0:T(8,128)(2,1)S(1)}, u32[]{:S(2)}, u32[]{:S(2)}) collective-permute-start(bf16[1,2,64,512]{3,2,1,0:T(8,128)(2,1)S(1)} %collective-permute-done.4), channel_id=1, source_target_pairs={{0,1},{1,2},{2,3},{3,4},{4,5},{5,6},{6,7},{7,0},{8,9},{9,10},{10,1... | collective-permute-start | bytes 393224 | tf_op jit(solution)/shard_map/ppermute | solution.py:52
  38.5 7.2 %collective-permute-start.8 = (bf16[1,2,64,512]{3,2,1,0:T(8,128)(2,1)S(1)}, bf16[1,2,64,512]{3,2,1,0:T(8,128)(2,1)S(1)}, u32[]{:S(2)}, u32[]{:S(2)}) collective-permute-start(bf16[1,2,64,512]{3,2,1,0:T(8,128)(2,1)S(1)} %collective-permute-done.6), channel_id=1, source_target_pairs={{0,1},{1,2},{2,3},{3,4},{4,5},{5,6},{6,7},{7,0},{8,9},{9,10},{10,1... | collective-permute-start | bytes 393224 | tf_op jit(solution)/shard_map/ppermute | solution.py:52
  61.2 36.6 %copy-start = (bf16[40,128,256]{2,1,0:T(8,128)(2,1)}, bf16[40,128,256]{2,1,0:T(8,128)(2,1)S(1)}, u32[]{:S(2)}) copy-start(bf16[40,128,256]{2,1,0:T(8,128)(2,1)S(1)} %get-tuple-element.43) | copy-start | bytes 7864324
  97.8 8.2 %copy-start.6 = (f32[9,2048]{1,0:T(8,128)S(1)}, f32[9,2048]{1,0:T(8,128)}, u32[]{:S(2)}) copy-start(f32[9,2048]{1,0:T(8,128)} %param.12) | copy-start | bytes 221188
  100.3 7.7 %collective-permute-start = (bf16[1,1,64,2048]{3,2,1,0:T(8,128)(2,1)S(1)}, bf16[1,1,64,2048]{3,2,1,0:T(8,128)(2,1)S(1)}, u32[]{:S(2)}, u32[]{:S(2)}) collective-permute-start(bf16[1,1,64,2048]{3,2,1,0:T(8,128)(2,1)S(1)} %get-tuple-element.32), channel_id=1, source_target_pairs={{0,8},{8,16},{16,24},{24,32},{32,40},{40,48},{48,56},{56,64},{64,7... | collective-permute-start | bytes 786440 | tf_op jit(solution)/shard_map/ppermute | solution.py:18
  102.4 8.8 %collective-permute-start.1 = (bf16[1,1,64,2048]{3,2,1,0:T(8,128)(2,1)S(1)}, bf16[1,1,64,2048]{3,2,1,0:T(8,128)(2,1)S(1)}, u32[]{:S(2)}, u32[]{:S(2)}) collective-permute-start(bf16[1,1,64,2048]{3,2,1,0:T(8,128)(2,1)S(1)} %get-tuple-element.33), channel_id=1, source_target_pairs={{8,0},{16,8},{24,16},{32,24},{40,32},{48,40},{56,48},{64,56},{72,6... | collective-permute-start | bytes 786440 | tf_op jit(solution)/shard_map/ppermute | solution.py:19
  111.4 28.6 %copy-start.2 = (bf16[40,128,256]{2,1,0:T(8,128)(2,1)S(1)}, bf16[40,128,256]{2,1,0:T(8,128)(2,1)}, u32[]{:S(2)}) copy-start(bf16[40,128,256]{2,1,0:T(8,128)(2,1)} %get-tuple-element.44) | copy-start | bytes 7864324
  149.3 8.2 %collective-permute-start.9 = (bf16[1,1,64,2048]{3,2,1,0:T(8,128)(2,1)S(1)}, bf16[1,1,64,2048]{3,2,1,0:T(8,128)(2,1)S(1)}, u32[]{:S(2)}, u32[]{:S(2)}) collective-permute-start(bf16[1,1,64,2048]{3,2,1,0:T(8,128)(2,1)S(1)} %get-tuple-element.30), channel_id=1, source_target_pairs={{0,8},{8,16},{16,24},{24,32},{32,40},{40,48},{48,56},{56,64},{64,7... | collective-permute-start | bytes 786440 | tf_op jit(solution)/shard_map/ppermute | solution.py:18
  151.5 7.3 %collective-permute-start.10 = (bf16[1,1,64,2048]{3,2,1,0:T(8,128)(2,1)S(1)}, bf16[1,1,64,2048]{3,2,1,0:T(8,128)(2,1)S(1)}, u32[]{:S(2)}, u32[]{:S(2)}) collective-permute-start(bf16[1,1,64,2048]{3,2,1,0:T(8,128)(2,1)S(1)} %get-tuple-element.31), channel_id=1, source_target_pairs={{8,0},{16,8},{24,16},{32,24},{40,32},{48,40},{56,48},{64,56},{72,6... | collective-permute-start | bytes 786440 | tf_op jit(solution)/shard_map/ppermute | solution.py:19
  154.9 3.9 %copy-start.3 = (bf16[1,2,64,2048]{3,2,1,0:T(8,128)(2,1)S(1)}, bf16[1,2,64,2048]{3,2,1,0:T(8,128)(2,1)}, u32[]{:S(2)}) copy-start(bf16[1,2,64,2048]{3,2,1,0:T(8,128)(2,1)} %reshape.189) | copy-start | bytes 1572868
  159.0 1.7 copy-start.1
  183.3 0.7 copy-start.7
  183.3 1.1 copy-start.4
  183.3 151.9 %reduce-scatter.3.cloned.1.call-start = ((), (), s32[]{:S(2)}) async-start(), calls=%async_computation.5 | async-start | bytes 1179648 | tf_op jit(solution)/shard_map/reduce_scatter | solution.py:119
Sparse Core Ops, SparseCore 0:
  9.8 42.4 all-gather.3
  54.7 38.7 all-gather.5
  95.9 44.0 all-gather.7
  183.5 110.2 reduce-scatter.4
  296.8 38.3 reduce-scatter.2
